TPU v7x, 768 devices: a whole 4x8x12 slice. The times are simulated.
768 devices in a mesh: dp: 8 (over x, core), segment: 8 (over y), seq: 12 (over z).
Axes of the slice: x: 4, y: 8, z: 12, core: 2. Of those that a mesh axis runs over, the one named last changes fastest.
Arguments:
- activations: bfloat16 [8, 4, 1536, 768], P('dp', None, 'seq'), may hold values from -6 to 6
- conv_weight: bfloat16 [8, 5, 768, 768], P('segment', None, ('dp', 'seq')), may hold values from -0.125 to 0.125
- norm_gain: float32 [8, 768], P('segment'), may hold values from 0.25 to 1.75
- conv_bias: float32 [8, 768], P('segment'), may hold values from -3 to 3
Outputs:
- block_outputs: bfloat16 [8, 8, 4, 1536, 768], P('segment', 'dp', None, 'seq')
All inputs are finite; a program needn't handle non-finite values.
Results may differ from a plain program's by a relative error of at most 0.0065.
Values may be sent and summed in bfloat16 or wider, within the bound.
No kernel may reach another device: no remote copies, remote signals or barrier semaphores. Data moves between devices by JAX's collectives and lax.ppermute only.
A program may use at most 32 MiB of HBM per device.

v0:
```python
import jax
import jax.numpy as jnp
from jax import lax
from jax.experimental import pallas as pl
from jax.experimental.pallas import tpu as pltpu
from jax.sharding import Mesh, PartitionSpec as P


PAIR = 2


def shifted(block, axis, distance):
    count = lax.axis_size(axis)
    return lax.ppermute(block, axis, [(i, (i + distance) % count) for i in range(count)])


def moved(block, axis, distance):
    devices = range(lax.axis_size(axis))
    return lax.ppermute(block, axis, [(i, i + distance) for i in devices if i + distance in devices])


def merge_kernel(counts, *refs):
    sources, target, sems = refs[:-2], refs[-2], refs[-1]
    copies, at = [], 0
    for index, count in enumerate(counts):
        copies.append(pltpu.make_async_copy(sources[index], target.at[at : at + count], sems.at[index]))
        at += count
    for copy in copies:
        copy.start()
    for copy in copies:
        copy.wait()


def merged(blocks):
    counts = [block.shape[0] for block in blocks]
    return pl.pallas_call(
        lambda *refs: merge_kernel(counts, *refs),
        out_shape=jax.ShapeDtypeStruct((sum(counts),) + blocks[0].shape[1:], blocks[0].dtype),
        in_specs=[pl.BlockSpec(memory_space=pl.ANY)] * len(blocks),
        out_specs=pl.BlockSpec(memory_space=pltpu.VMEM),
        scratch_shapes=[pltpu.SemaphoreType.DMA((len(blocks),))],
        compiler_params=pltpu.CompilerParams(vmem_limit_bytes=8 << 20),
        name="merge",
    )(*blocks)


def assemble_kernel(pieces, taps, group, where_ref, *refs):
    sources, target, sems = refs[:-2], refs[-2], refs[-1]
    copies = []
    for at, (source, skip, row, first, count) in enumerate(pieces):
        base = where_ref[row] * group + first
        for tap in range(taps):
            copies.append(
                pltpu.make_async_copy(
                    sources[source].at[skip : skip + count, tap],
                    target.at[tap, pl.ds(base, count)],
                    sems.at[at * taps + tap],
                )
            )
    for copy in copies:
        copy.start()
    for copy in copies:
        copy.wait()


def gathered(shard, places):
    taps, rows, width = shard.shape
    group = lax.axis_size("seq")
    half = group // 2
    across = lax.axis_size("x")
    own = lax.all_gather(shard.reshape(1, taps * rows, width), "seq", axis=0, tiled=True)
    low, high = own[:half], own[half:]
    left_low, left_high = shifted(low, "x", 1), shifted(high, "x", 1)
    right_high, right_low = shifted(high, "x", -1), shifted(low, "x", -1)
    far_low = shifted(left_low, "x", 1)
    far_high = shifted(right_high, "x", -1)
    parts = [
        (own, 0, 0),
        (left_low, 3, 0),
        (left_high, 3, half),
        (right_low, 1, 0),
        (right_high, 1, half),
        (far_low, 2, 0),
        (far_high, 2, half),
    ]
    arrays, pieces = [], []
    for block, offset, first in parts:
        pieces.append((len(arrays), 0, offset, first, block.shape[0]))
        arrays.append(block)
    for some in (parts[:5], parts[5:]):
        skip = 0
        for block, offset, first in some:
            pieces.append((len(arrays), skip, across + offset, first, block.shape[0]))
            skip += block.shape[0]
        both = merged([part[0] for part in some])
        arrays.append(shifted(both, "core", 1))
    blocks = across * 2 * group
    out = pl.pallas_call(
        lambda *refs: assemble_kernel(pieces, taps, group, *refs),
        out_shape=jax.ShapeDtypeStruct((taps, blocks, rows, width), shard.dtype),
        in_specs=[pl.BlockSpec(memory_space=pltpu.SMEM)]
        + [pl.BlockSpec(memory_space=pl.ANY)] * len(arrays),
        out_specs=pl.BlockSpec(memory_space=pltpu.VMEM),
        scratch_shapes=[pltpu.SemaphoreType.DMA((len(pieces) * taps,))],
        compiler_params=pltpu.CompilerParams(vmem_limit_bytes=16 << 20),
        name="assemble",
    )(places, *[array.reshape(-1, taps, rows, width) for array in arrays])
    return out.reshape(taps * blocks * rows, width)


def block_kernel(turn, pairs, segments, taps, length, halo, has_own, has_incoming, has_join, info_ref, *refs):
    refs = list(refs)
    incoming_ref = refs.pop(0) if has_incoming else None
    own_ref = refs.pop(0) if has_own else None
    join_ref = refs.pop(0) if has_join else None
    kernel_ref, gain_ref, bias_ref, out_ref, cat_ref = refs
    extent, width = out_ref.shape
    segment = info_ref[0]
    pair = turn - segment

    @pl.when(jnp.logical_and(pair >= 0, pair < pairs))
    def _():
        if has_own and has_incoming:
            pick = segment == 0
            wide = jnp.where(pick, own_ref[...].astype(jnp.float32), incoming_ref[...].astype(jnp.float32))
        else:
            wide = (own_ref if has_own else incoming_ref)[...].astype(jnp.float32)
        stat = jnp.mean(wide * wide, axis=-1, keepdims=True)
        place = info_ref[1] + lax.broadcasted_iota(jnp.int32, (extent, 1), 0)
        inside = jnp.logical_and(place >= 0, place < length)
        normed = wide * lax.rsqrt(stat + 1e-06) * gain_ref[...]
        normed = jnp.where(inside, normed, 0.0)
        for tap in range(taps):
            back = (taps // 2 - tap) % extent
            turned = pltpu.roll(normed, back, 0) if back else normed
            cat_ref[:, tap * width : (tap + 1) * width] = turned.astype(jnp.bfloat16)
        total = jnp.dot(cat_ref[...], kernel_ref[...], preferred_element_type=jnp.float32)
        lifted = wide + jax.nn.gelu(total + bias_ref[...], approximate=True)
        out_ref[...] = lifted.astype(jnp.bfloat16)
        if has_join:

            @pl.when(segment == segments - 1)
            def _():
                inner = lifted[halo : extent - halo] + join_ref[...].astype(jnp.float32)
                out_ref[halo : extent - halo, :] = inner.astype(jnp.bfloat16)


def block(info, incoming, own, join, kernel, gain, bias, turn, pairs, segments, taps, length, halo):
    given = [a for a in (incoming, own, join) if a is not None]
    extent, width = (incoming if incoming is not None else own).shape
    vmem = pl.BlockSpec(memory_space=pltpu.VMEM)
    return pl.pallas_call(
        lambda *refs: block_kernel(
            turn, pairs, segments, taps, length, halo, own is not None, incoming is not None, join is not None, *refs
        ),
        out_shape=jax.ShapeDtypeStruct((extent, width), jnp.bfloat16),
        in_specs=[pl.BlockSpec(memory_space=pltpu.SMEM)] + [vmem] * (len(given) + 3),
        out_specs=vmem,
        scratch_shapes=[pltpu.VMEM((extent, taps * width), jnp.bfloat16)],
        compiler_params=pltpu.CompilerParams(vmem_limit_bytes=16 << 20),
        cost_estimate=pl.CostEstimate(
            flops=2 * extent * taps * width * width,
            bytes_accessed=2 * taps * width * width,
            transcendentals=extent * width,
        ),
        name="block",
    )(info, *given, kernel, gain, bias)


def per_device(activations, conv_weight, norm_gain, conv_bias):
    inputs = activations[0]
    micro_count, rows, _ = inputs.shape
    segments = lax.axis_size("segment")
    segment = lax.axis_index("segment")
    seq = lax.axis_index("seq")
    taps = conv_weight.shape[1]
    halo = segments * (taps // 2)
    length = rows * lax.axis_size("seq")

    before = moved(inputs[:, rows - halo :], "seq", 1)
    after = moved(inputs[:, :halo], "seq", -1)
    extended = jnp.concatenate([before, inputs, after], axis=1)
    pairs = micro_count // PAIR
    turns = segments + pairs - 1
    x, core, across = lax.axis_index("x"), lax.axis_index("core"), lax.axis_size("x")
    order = lax.rem(x + jnp.arange(across, dtype=jnp.int32), across) * 2
    places = jnp.concatenate([order + core, order + 1 - core])
    info = jnp.stack([segment, seq * rows - halo]).astype(jnp.int32)
    owns = [[turn - segment == which for turn in range(turns)] for which in range(pairs)]
    owns, info, places, shard = lax.optimization_barrier((owns, info, places, conv_weight[0]))
    kernel = gathered(shard, places)
    incoming = [None] * PAIR
    kept = [None] * micro_count
    early = []
    joined = None
    for turn in range(turns):
        for lane in range(PAIR):
            own = extended[turn * PAIR + lane] if turn < pairs else None
            join = joined[(turn - segments + 1) * PAIR + lane] if turn >= segments - 1 else None
            out = block(info, incoming[lane], own, join, kernel, norm_gain, conv_bias, turn, pairs, segments, taps, length, halo)
            if turn < turns - 1:
                incoming[lane] = moved(out, "segment", 1)
            inner = out[halo : halo + rows]
            if turn < pairs:
                early.append(inner)
            for which in range(pairs):
                if which <= turn < segments + which:
                    at = which * PAIR + lane
                    kept[at] = inner if kept[at] is None else jnp.where(owns[which][turn], inner, kept[at])
        if turn == pairs - 1:
            joined = lax.ppermute(jnp.stack(early), "segment", [(0, segments - 1)])
    return jnp.stack(kept)[None, None]


def solution(mesh):
    dp, segments, seq = (mesh.shape[name] for name in ("dp", "segment", "seq"))
    split = Mesh(mesh.devices.reshape(dp // 2, 2, segments, seq), ("x", "core", "segment", "seq"))
    in_specs = (
        P(("x", "core"), None, "seq", None),
        P("segment", None, ("x", "core", "seq"), None),
        P("segment", None),
        P("segment", None),
    )
    out_specs = P("segment", ("x", "core"), None, "seq", None)

    return jax.shard_map(per_device, mesh=split, in_specs=in_specs, out_specs=out_specs, check_vma=False)
```

profile of v0, /device:TPU:38, one launch (start us, length us, event | category | flops | bytes accessed | tf_op | source)
XLA Modules:
  0.0 192.6 jit_solution(3286750171551550815)
XLA Ops:
  0.2 36.9 %all_gather.3.refs_0_ = bf16[12,40,768]{2,1,0:T(8,128)(2,1)S(1)} all-gather(bf16[1,40,768]{2,1,0:T(8,128)(2,1)} %bitcast.78), channel_id=1, replica_groups=mesh['x'=4,'core'=2,'segment'=8,'seq'=12] {'seq'}, dimensions={0}, use_global_device_ids=true | all-gather | bytes 798720 | tf_op jit(solution)/shard_map/all_gather | solution.py:71
  37.2 2.4 %collective-permute-start.2 = (bf16[6,40,768]{2,1,0:T(8,128)(2,1)S(1)}, bf16[6,40,768]{2,1,0:T(8,128)(2,1)S(1)}, u32[]{:S(2)}, u32[]{:S(2)}) collective-permute-start(bf16[6,40,768]{2,1,0:T(8,128)(2,1)S(1)} %get-tuple-element.50), channel_id=1, source_target_pairs={{0,192},{192,384},{384,576},{576,0},{1,193},{193,385},{385,577},{5... | collective-permute-start | bytes 1105928 | tf_op jit(solution)/shard_map/ppermute | solution.py:14
  39.6 3.5 %collective-permute-start.3 = (bf16[6,40,768]{2,1,0:T(8,128)(2,1)S(1)}, bf16[6,40,768]{2,1,0:T(8,128)(2,1)S(1)}, u32[]{:S(2)}, u32[]{:S(2)}) collective-permute-start(bf16[6,40,768]{2,1,0:T(8,128)(2,1)S(1)} %get-tuple-element.49), channel_id=1, source_target_pairs={{0,192},{192,384},{384,576},{576,0},{1,193},{193,385},{385,577},{5... | collective-permute-start | bytes 1105928 | tf_op jit(solution)/shard_map/ppermute | solution.py:14
  43.1 2.4 %collective-permute-start.4 = (bf16[6,40,768]{2,1,0:T(8,128)(2,1)S(1)}, bf16[6,40,768]{2,1,0:T(8,128)(2,1)S(1)}, u32[]{:S(2)}, u32[]{:S(2)}) collective-permute-start(bf16[6,40,768]{2,1,0:T(8,128)(2,1)S(1)} %get-tuple-element.50), channel_id=1, source_target_pairs={{0,576},{192,0},{384,192},{576,384},{1,577},{193,1},{385,193},{577... | collective-permute-start | bytes 1105928 | tf_op jit(solution)/shard_map/ppermute | solution.py:14
  45.6 3.5 %collective-permute-start.5 = (bf16[6,40,768]{2,1,0:T(8,128)(2,1)S(1)}, bf16[6,40,768]{2,1,0:T(8,128)(2,1)S(1)}, u32[]{:S(2)}, u32[]{:S(2)}) collective-permute-start(bf16[6,40,768]{2,1,0:T(8,128)(2,1)S(1)} %get-tuple-element.49), channel_id=1, source_target_pairs={{0,576},{192,0},{384,192},{576,384},{1,577},{193,1},{385,193},{577... | collective-permute-start | bytes 1105928 | tf_op jit(solution)/shard_map/ppermute | solution.py:14
  49.0 3.0 %collective-permute-done.3.refs_2_ = bf16[6,40,768]{2,1,0:T(8,128)(2,1)S(1)} collective-permute-done((bf16[6,40,768]{2,1,0:T(8,128)(2,1)S(1)}, bf16[6,40,768]{2,1,0:T(8,128)(2,1)S(1)}, u32[]{:S(2)}, u32[]{:S(2)}) %collective-permute-start.3) | collective-permute-done | bytes 368672 | tf_op jit(solution)/shard_map/ppermute | solution.py:14
  52.0 2.6 %collective-permute-done.4.refs_3_ = bf16[6,40,768]{2,1,0:T(8,128)(2,1)S(1)} collective-permute-done((bf16[6,40,768]{2,1,0:T(8,128)(2,1)S(1)}, bf16[6,40,768]{2,1,0:T(8,128)(2,1)S(1)}, u32[]{:S(2)}, u32[]{:S(2)}) %collective-permute-start.4) | collective-permute-done | bytes 368672 | tf_op jit(solution)/shard_map/ppermute | solution.py:14
  54.7 3.9 %collective-permute-done.5.refs_4_ = bf16[6,40,768]{2,1,0:T(8,128)(2,1)S(1)} collective-permute-done((bf16[6,40,768]{2,1,0:T(8,128)(2,1)S(1)}, bf16[6,40,768]{2,1,0:T(8,128)(2,1)S(1)}, u32[]{:S(2)}, u32[]{:S(2)}) %collective-permute-start.5) | collective-permute-done | bytes 368672 | tf_op jit(solution)/shard_map/ppermute | solution.py:14
  59.6 1.9 collective-permute-start.8
  61.5 2.2 %collective-permute-start.6 = (bf16[6,40,768]{2,1,0:T(8,128)(2,1)S(1)}, bf16[6,40,768]{2,1,0:T(8,128)(2,1)S(1)}, u32[]{:S(2)}, u32[]{:S(2)}) collective-permute-start(bf16[6,40,768]{2,1,0:T(8,128)(2,1)S(1)} %collective-permute-done.2.refs_1_), channel_id=1, source_target_pairs={{0,192},{192,384},{384,576},{576,0},{1,193},{193,385},{385,577},{5... | collective-permute-start | bytes 1105928 | tf_op jit(solution)/shard_map/ppermute | solution.py:14
  63.7 3.7 %collective-permute-start.7 = (bf16[6,40,768]{2,1,0:T(8,128)(2,1)S(1)}, bf16[6,40,768]{2,1,0:T(8,128)(2,1)S(1)}, u32[]{:S(2)}, u32[]{:S(2)}) collective-permute-start(bf16[6,40,768]{2,1,0:T(8,128)(2,1)S(1)} %collective-permute-done.5.refs_4_), channel_id=1, source_target_pairs={{0,576},{192,0},{384,192},{576,384},{1,577},{193,1},{385,193},{577... | collective-permute-start | bytes 1105928 | tf_op jit(solution)/shard_map/ppermute | solution.py:14
  67.4 7.0 %collective-permute-done.6.refs_0_ = bf16[6,40,768]{2,1,0:T(8,128)(2,1)S(1)} collective-permute-done((bf16[6,40,768]{2,1,0:T(8,128)(2,1)S(1)}, bf16[6,40,768]{2,1,0:T(8,128)(2,1)S(1)}, u32[]{:S(2)}, u32[]{:S(2)}) %collective-permute-start.6) | collective-permute-done | bytes 368672 | tf_op jit(solution)/shard_map/ppermute | solution.py:14
  74.4 3.1 %collective-permute-done.7.refs_1_ = bf16[6,40,768]{2,1,0:T(8,128)(2,1)S(1)} collective-permute-done((bf16[6,40,768]{2,1,0:T(8,128)(2,1)S(1)}, bf16[6,40,768]{2,1,0:T(8,128)(2,1)S(1)}, u32[]{:S(2)}, u32[]{:S(2)}) %collective-permute-start.7) | collective-permute-done | bytes 368672 | tf_op jit(solution)/shard_map/ppermute | solution.py:14
  84.1 4.1 %collective-permute-done.1 = bf16[4,16,768]{2,1,0:T(8,128)(2,1)S(1)} collective-permute-done((bf16[4,16,768]{2,1,0:T(8,128)(2,1)S(1)}, bf16[4,16,768]{2,1,0:T(8,128)(2,1)S(1)}, u32[]{:S(2)}, u32[]{:S(2)}) %collective-permute-start.1) | collective-permute-done | bytes 98336 | tf_op jit(solution)/shard_map/ppermute | solution.py:19
  88.4 2.4 %assemble.1 = bf16[5,96,8,768]{3,2,1,0:T(8,128)(2,1)S(1)} custom-call(s32[8]{0:T(128)S(1)} %pad_add_fusion.1.refs_0_, bf16[12,5,8,768]{3,2,1,0:T(8,128)(2,1)S(1)} %bitcast.67, bf16[6,5,8,768]{3,2,1,0:T(8,128)(2,1)S(1)} %bitcast.69, bf16[6,5,8,768]{3,2,1,0:T(8,128)(2,1)S(1)} %bitcast.70, bf16[6,5,8,768]{3,2,1,0:T(8,128)(2,1)S(1)} %bitcast.71, ...), custom_call_target="tpu_custom_call" | custom-call | tf_op jit(solution)/shard_map/assemble/pallas_call | solution.py:98
  91.4 2.6 %collective-permute-start.10 = (bf16[160,768]{1,0:T(8,128)(2,1)S(1)}, bf16[160,768]{1,0:T(8,128)(2,1)S(1)}, u32[]{:S(2)}, u32[]{:S(2)}) collective-permute-start(bf16[160,768]{1,0:T(8,128)(2,1)S(1)} %block.18), channel_id=1, source_target_pairs={{0,12},{12,24},{24,36},{36,48},{48,60},{60,72},{72,84},{1,13},{13,... | collective-permute-start | bytes 737288 | tf_op jit(solution)/shard_map/ppermute | solution.py:19
  94.6 2.6 %collective-permute-start.17 = (bf16[160,768]{1,0:T(8,128)(2,1)S(1)}, bf16[160,768]{1,0:T(8,128)(2,1)S(1)}, u32[]{:S(2)}, u32[]{:S(2)}) collective-permute-start(bf16[160,768]{1,0:T(8,128)(2,1)S(1)} %block.25), channel_id=1, source_target_pairs={{0,12},{12,24},{24,36},{36,48},{48,60},{60,72},{72,84},{1,13},{13,... | collective-permute-start | bytes 737288 | tf_op jit(solution)/shard_map/ppermute | solution.py:19
  97.2 6.2 %collective-permute-done.10.refs_1_ = bf16[160,768]{1,0:T(8,128)(2,1)S(1)} collective-permute-done((bf16[160,768]{1,0:T(8,128)(2,1)S(1)}, bf16[160,768]{1,0:T(8,128)(2,1)S(1)}, u32[]{:S(2)}, u32[]{:S(2)}) %collective-permute-start.10) | collective-permute-done | bytes 245792 | tf_op jit(solution)/shard_map/ppermute | solution.py:19
  108.1 1.9 collective-permute-start.19
  110.0 4.1 %collective-permute-done.11.refs_1_ = bf16[160,768]{1,0:T(8,128)(2,1)S(1)} collective-permute-done((bf16[160,768]{1,0:T(8,128)(2,1)S(1)}, bf16[160,768]{1,0:T(8,128)(2,1)S(1)}, u32[]{:S(2)}, u32[]{:S(2)}) %collective-permute-start.11) | collective-permute-done | bytes 245792 | tf_op jit(solution)/shard_map/ppermute | solution.py:19
  116.6 3.4 %collective-permute-done.19.refs_1_ = bf16[160,768]{1,0:T(8,128)(2,1)S(1)} collective-permute-done((bf16[160,768]{1,0:T(8,128)(2,1)S(1)}, bf16[160,768]{1,0:T(8,128)(2,1)S(1)}, u32[]{:S(2)}, u32[]{:S(2)}) %collective-permute-start.19) | collective-permute-done | bytes 245792 | tf_op jit(solution)/shard_map/ppermute | solution.py:19
  122.5 2.1 %collective-permute-done.12.refs_1_ = bf16[160,768]{1,0:T(8,128)(2,1)S(1)} collective-permute-done((bf16[160,768]{1,0:T(8,128)(2,1)S(1)}, bf16[160,768]{1,0:T(8,128)(2,1)S(1)}, u32[]{:S(2)}, u32[]{:S(2)}) %collective-permute-start.12) | collective-permute-done | bytes 245792 | tf_op jit(solution)/shard_map/ppermute | solution.py:19
  127.1 5.4 %collective-permute-done.20.refs_1_ = bf16[160,768]{1,0:T(8,128)(2,1)S(1)} collective-permute-done((bf16[160,768]{1,0:T(8,128)(2,1)S(1)}, bf16[160,768]{1,0:T(8,128)(2,1)S(1)}, u32[]{:S(2)}, u32[]{:S(2)}) %collective-permute-start.20) | collective-permute-done | bytes 245792 | tf_op jit(solution)/shard_map/ppermute | solution.py:19
  141.1 3.7 %collective-permute-done.21.refs_1_ = bf16[160,768]{1,0:T(8,128)(2,1)S(1)} collective-permute-done((bf16[160,768]{1,0:T(8,128)(2,1)S(1)}, bf16[160,768]{1,0:T(8,128)(2,1)S(1)}, u32[]{:S(2)}, u32[]{:S(2)}) %collective-permute-start.21) | collective-permute-done | bytes 245792 | tf_op jit(solution)/shard_map/ppermute | solution.py:19
  154.2 4.2 %collective-permute-done.22.refs_1_ = bf16[160,768]{1,0:T(8,128)(2,1)S(1)} collective-permute-done((bf16[160,768]{1,0:T(8,128)(2,1)S(1)}, bf16[160,768]{1,0:T(8,128)(2,1)S(1)}, u32[]{:S(2)}, u32[]{:S(2)}) %collective-permute-start.22) | collective-permute-done | bytes 245792 | tf_op jit(solution)/shard_map/ppermute | solution.py:19
  160.2 1.9 collective-permute-start.23
  163.7 2.3 %collective-permute-start.16 = (bf16[160,768]{1,0:T(8,128)(2,1)S(1)}, bf16[160,768]{1,0:T(8,128)(2,1)S(1)}, u32[]{:S(2)}, u32[]{:S(2)}) collective-permute-start(bf16[160,768]{1,0:T(8,128)(2,1)S(1)} %block.24), channel_id=1, source_target_pairs={{0,12},{12,24},{24,36},{36,48},{48,60},{60,72},{72,84},{1,13},{13,... | collective-permute-start | bytes 737288 | tf_op jit(solution)/shard_map/ppermute | solution.py:19
  166.0 4.7 %collective-permute-done.23.refs_1_ = bf16[160,768]{1,0:T(8,128)(2,1)S(1)} collective-permute-done((bf16[160,768]{1,0:T(8,128)(2,1)S(1)}, bf16[160,768]{1,0:T(8,128)(2,1)S(1)}, u32[]{:S(2)}, u32[]{:S(2)}) %collective-permute-start.23) | collective-permute-done | bytes 245792 | tf_op jit(solution)/shard_map/ppermute | solution.py:19
  173.3 2.7 %collective-permute-done.16.refs_1_ = bf16[160,768]{1,0:T(8,128)(2,1)S(1)} collective-permute-done((bf16[160,768]{1,0:T(8,128)(2,1)S(1)}, bf16[160,768]{1,0:T(8,128)(2,1)S(1)}, u32[]{:S(2)}, u32[]{:S(2)}) %collective-permute-start.16) | collective-permute-done | bytes 245792 | tf_op jit(solution)/shard_map/ppermute | solution.py:19
  178.5 2.7 %collective-permute-done.24.refs_1_ = bf16[160,768]{1,0:T(8,128)(2,1)S(1)} collective-permute-done((bf16[160,768]{1,0:T(8,128)(2,1)S(1)}, bf16[160,768]{1,0:T(8,128)(2,1)S(1)}, u32[]{:S(2)}, u32[]{:S(2)}) %collective-permute-start.24) | collective-permute-done | bytes 245792 | tf_op jit(solution)/shard_map/ppermute | solution.py:19
  181.7 2.1 %collective-permute-start.26 = (bf16[160,768]{1,0:T(8,128)(2,1)S(1)}, bf16[160,768]{1,0:T(8,128)(2,1)S(1)}, u32[]{:S(2)}, u32[]{:S(2)}) collective-permute-start(bf16[160,768]{1,0:T(8,128)(2,1)S(1)} %block.33), channel_id=1, source_target_pairs={{0,12},{12,24},{24,36},{36,48},{48,60},{60,72},{72,84},{1,13},{13,... | collective-permute-start | bytes 737288 | tf_op jit(solution)/shard_map/ppermute | solution.py:19
  186.5 4.5 %collective-permute-done.26.refs_1_ = bf16[160,768]{1,0:T(8,128)(2,1)S(1)} collective-permute-done((bf16[160,768]{1,0:T(8,128)(2,1)S(1)}, bf16[160,768]{1,0:T(8,128)(2,1)S(1)}, u32[]{:S(2)}, u32[]{:S(2)}) %collective-permute-start.26) | collective-permute-done | bytes 245792 | tf_op jit(solution)/shard_map/ppermute | solution.py:19
  (68 shorter events, 52.2 us)
Async XLA Ops:
  37.2 11.9 %collective-permute-start.2 = (bf16[6,40,768]{2,1,0:T(8,128)(2,1)S(1)}, bf16[6,40,768]{2,1,0:T(8,128)(2,1)S(1)}, u32[]{:S(2)}, u32[]{:S(2)}) collective-permute-start(bf16[6,40,768]{2,1,0:T(8,128)(2,1)S(1)} %get-tuple-element.50), channel_id=1, source_target_pairs={{0,192},{192,384},{384,576},{576,0},{1,193},{193,385},{385,577},{5... | collective-permute-start | bytes 1105928 | tf_op jit(solution)/shard_map/ppermute | solution.py:14
  39.5 40.3 %copy-start.2 = (bf16[1,4,128,768]{3,2,1,0:T(8,128)(2,1)S(1)}, bf16[1,4,128,768]{3,2,1,0:T(8,128)(2,1)}, u32[]{:S(2)}) copy-start(bf16[1,4,128,768]{3,2,1,0:T(8,128)(2,1)} %param.4) | copy-start | bytes 2359300
  39.6 12.5 %collective-permute-start.3 = (bf16[6,40,768]{2,1,0:T(8,128)(2,1)S(1)}, bf16[6,40,768]{2,1,0:T(8,128)(2,1)S(1)}, u32[]{:S(2)}, u32[]{:S(2)}) collective-permute-start(bf16[6,40,768]{2,1,0:T(8,128)(2,1)S(1)} %get-tuple-element.49), channel_id=1, source_target_pairs={{0,192},{192,384},{384,576},{576,0},{1,193},{193,385},{385,577},{5... | collective-permute-start | bytes 1105928 | tf_op jit(solution)/shard_map/ppermute | solution.py:14
  43.1 11.6 %collective-permute-start.4 = (bf16[6,40,768]{2,1,0:T(8,128)(2,1)S(1)}, bf16[6,40,768]{2,1,0:T(8,128)(2,1)S(1)}, u32[]{:S(2)}, u32[]{:S(2)}) collective-permute-start(bf16[6,40,768]{2,1,0:T(8,128)(2,1)S(1)} %get-tuple-element.50), channel_id=1, source_target_pairs={{0,576},{192,0},{384,192},{576,384},{1,577},{193,1},{385,193},{577... | collective-permute-start | bytes 1105928 | tf_op jit(solution)/shard_map/ppermute | solution.py:14
  45.6 13.1 %collective-permute-start.5 = (bf16[6,40,768]{2,1,0:T(8,128)(2,1)S(1)}, bf16[6,40,768]{2,1,0:T(8,128)(2,1)S(1)}, u32[]{:S(2)}, u32[]{:S(2)}) collective-permute-start(bf16[6,40,768]{2,1,0:T(8,128)(2,1)S(1)} %get-tuple-element.49), channel_id=1, source_target_pairs={{0,576},{192,0},{384,192},{576,384},{1,577},{193,1},{385,193},{577... | collective-permute-start | bytes 1105928 | tf_op jit(solution)/shard_map/ppermute | solution.py:14
  59.6 28.8 %collective-permute-start.8 = (bf16[36,40,768]{2,1,0:T(8,128)(2,1)S(1)}, bf16[36,40,768]{2,1,0:T(8,128)(2,1)S(1)}, u32[]{:S(2)}, u32[]{:S(2)}) collective-permute-start(bf16[36,40,768]{2,1,0:T(8,128)(2,1)S(1)} %merge.2), channel_id=1, source_target_pairs={{0,96},{96,0},{1,97},{97,1},{2,98},{98,2},{3,99},{99,3},{4,100},{1... | collective-permute-start | bytes 6635528 | tf_op jit(solution)/shard_map/ppermute | solution.py:14
  61.5 12.9 %collective-permute-start.6 = (bf16[6,40,768]{2,1,0:T(8,128)(2,1)S(1)}, bf16[6,40,768]{2,1,0:T(8,128)(2,1)S(1)}, u32[]{:S(2)}, u32[]{:S(2)}) collective-permute-start(bf16[6,40,768]{2,1,0:T(8,128)(2,1)S(1)} %collective-permute-done.2.refs_1_), channel_id=1, source_target_pairs={{0,192},{192,384},{384,576},{576,0},{1,193},{193,385},{385,577},{5... | collective-permute-start | bytes 1105928 | tf_op jit(solution)/shard_map/ppermute | solution.py:14
  63.7 13.8 %collective-permute-start.7 = (bf16[6,40,768]{2,1,0:T(8,128)(2,1)S(1)}, bf16[6,40,768]{2,1,0:T(8,128)(2,1)S(1)}, u32[]{:S(2)}, u32[]{:S(2)}) collective-permute-start(bf16[6,40,768]{2,1,0:T(8,128)(2,1)S(1)} %collective-permute-done.5.refs_4_), channel_id=1, source_target_pairs={{0,576},{192,0},{384,192},{576,384},{1,577},{193,1},{385,193},{577... | collective-permute-start | bytes 1105928 | tf_op jit(solution)/shard_map/ppermute | solution.py:14
  77.9 10.5 %collective-permute-start.9 = (bf16[12,40,768]{2,1,0:T(8,128)(2,1)S(1)}, bf16[12,40,768]{2,1,0:T(8,128)(2,1)S(1)}, u32[]{:S(2)}, u32[]{:S(2)}) collective-permute-start(bf16[12,40,768]{2,1,0:T(8,128)(2,1)S(1)} %merge.3), channel_id=1, source_target_pairs={{0,96},{96,0},{1,97},{97,1},{2,98},{98,2},{3,99},{99,3},{4,100},{1... | collective-permute-start | bytes 2211848 | tf_op jit(solution)/shard_map/ppermute | solution.py:14
  79.8 4.3 %collective-permute-start = (bf16[4,16,768]{2,1,0:T(8,128)(2,1)S(1)}, bf16[4,16,768]{2,1,0:T(8,128)(2,1)S(1)}, u32[]{:S(2)}, u32[]{:S(2)}) collective-permute-start(bf16[4,16,768]{2,1,0:T(8,128)(2,1)S(1)} %get-tuple-element.47), channel_id=1, source_target_pairs={{0,1},{1,2},{2,3},{3,4},{4,5},{5,6},{6,7},{7,8},{8,9},{9,10},{10,1... | collective-permute-start | bytes 294920 | tf_op jit(solution)/shard_map/ppermute | solution.py:19
  81.2 7.1 %collective-permute-start.1 = (bf16[4,16,768]{2,1,0:T(8,128)(2,1)S(1)}, bf16[4,16,768]{2,1,0:T(8,128)(2,1)S(1)}, u32[]{:S(2)}, u32[]{:S(2)}) collective-permute-start(bf16[4,16,768]{2,1,0:T(8,128)(2,1)S(1)} %get-tuple-element.48), channel_id=1, source_target_pairs={{1,0},{2,1},{3,2},{4,3},{5,4},{6,5},{7,6},{8,7},{9,8},{10,9},{11,1... | collective-permute-start | bytes 294920 | tf_op jit(solution)/shard_map/ppermute | solution.py:19
  88.4 2.4 %copy-start = (f32[1,768]{1,0:T(1,128)S(1)}, f32[1,768]{1,0:T(1,128)}, u32[]{:S(2)}) copy-start(f32[1,768]{1,0:T(1,128)} %refs_4_.35) | copy-start | bytes 9220
  88.4 2.4 %copy-start.1 = (f32[1,768]{1,0:T(1,128)S(1)}, f32[1,768]{1,0:T(1,128)}, u32[]{:S(2)}) copy-start(f32[1,768]{1,0:T(1,128)} %refs_5_.11) | copy-start | bytes 9220
  91.4 11.9 %collective-permute-start.10 = (bf16[160,768]{1,0:T(8,128)(2,1)S(1)}, bf16[160,768]{1,0:T(8,128)(2,1)S(1)}, u32[]{:S(2)}, u32[]{:S(2)}) collective-permute-start(bf16[160,768]{1,0:T(8,128)(2,1)S(1)} %block.18), channel_id=1, source_target_pairs={{0,12},{12,24},{24,36},{36,48},{48,60},{60,72},{72,84},{1,13},{13,... | collective-permute-start | bytes 737288 | tf_op jit(solution)/shard_map/ppermute | solution.py:19
  94.6 12.9 %collective-permute-start.17 = (bf16[160,768]{1,0:T(8,128)(2,1)S(1)}, bf16[160,768]{1,0:T(8,128)(2,1)S(1)}, u32[]{:S(2)}, u32[]{:S(2)}) collective-permute-start(bf16[160,768]{1,0:T(8,128)(2,1)S(1)} %block.25), channel_id=1, source_target_pairs={{0,12},{12,24},{24,36},{36,48},{48,60},{60,72},{72,84},{1,13},{13,... | collective-permute-start | bytes 737288 | tf_op jit(solution)/shard_map/ppermute | solution.py:19
  103.9 10.2 %collective-permute-start.11 = (bf16[160,768]{1,0:T(8,128)(2,1)S(1)}, bf16[160,768]{1,0:T(8,128)(2,1)S(1)}, u32[]{:S(2)}, u32[]{:S(2)}) collective-permute-start(bf16[160,768]{1,0:T(8,128)(2,1)S(1)} %block.19), channel_id=1, source_target_pairs={{0,12},{12,24},{24,36},{36,48},{48,60},{60,72},{72,84},{1,13},{13,... | collective-permute-start | bytes 737288 | tf_op jit(solution)/shard_map/ppermute | solution.py:19
  108.1 11.9 %collective-permute-start.19 = (bf16[160,768]{1,0:T(8,128)(2,1)S(1)}, bf16[160,768]{1,0:T(8,128)(2,1)S(1)}, u32[]{:S(2)}, u32[]{:S(2)}) collective-permute-start(bf16[160,768]{1,0:T(8,128)(2,1)S(1)} %block.26), channel_id=1, source_target_pairs={{0,12},{12,24},{24,36},{36,48},{48,60},{60,72},{72,84},{1,13},{13,... | collective-permute-start | bytes 737288 | tf_op jit(solution)/shard_map/ppermute | solution.py:19
  114.6 9.9 %collective-permute-start.12 = (bf16[160,768]{1,0:T(8,128)(2,1)S(1)}, bf16[160,768]{1,0:T(8,128)(2,1)S(1)}, u32[]{:S(2)}, u32[]{:S(2)}) collective-permute-start(bf16[160,768]{1,0:T(8,128)(2,1)S(1)} %block.20), channel_id=1, source_target_pairs={{0,12},{12,24},{24,36},{36,48},{48,60},{60,72},{72,84},{1,13},{13,... | collective-permute-start | bytes 737288 | tf_op jit(solution)/shard_map/ppermute | solution.py:19
  120.6 11.9 %collective-permute-start.20 = (bf16[160,768]{1,0:T(8,128)(2,1)S(1)}, bf16[160,768]{1,0:T(8,128)(2,1)S(1)}, u32[]{:S(2)}, u32[]{:S(2)}) collective-permute-start(bf16[160,768]{1,0:T(8,128)(2,1)S(1)} %block.28), channel_id=1, source_target_pairs={{0,12},{12,24},{24,36},{36,48},{48,60},{60,72},{72,84},{1,13},{13,... | collective-permute-start | bytes 737288 | tf_op jit(solution)/shard_map/ppermute | solution.py:19
  125.1 12.2 %collective-permute-start.13 = (bf16[160,768]{1,0:T(8,128)(2,1)S(1)}, bf16[160,768]{1,0:T(8,128)(2,1)S(1)}, u32[]{:S(2)}, u32[]{:S(2)}) collective-permute-start(bf16[160,768]{1,0:T(8,128)(2,1)S(1)} %block.21), channel_id=1, source_target_pairs={{0,12},{12,24},{24,36},{36,48},{48,60},{60,72},{72,84},{1,13},{13,... | collective-permute-start | bytes 737288 | tf_op jit(solution)/shard_map/ppermute | solution.py:19
  133.2 11.7 %collective-permute-start.21 = (bf16[160,768]{1,0:T(8,128)(2,1)S(1)}, bf16[160,768]{1,0:T(8,128)(2,1)S(1)}, u32[]{:S(2)}, u32[]{:S(2)}) collective-permute-start(bf16[160,768]{1,0:T(8,128)(2,1)S(1)} %block.29), channel_id=1, source_target_pairs={{0,12},{12,24},{24,36},{36,48},{48,60},{60,72},{72,84},{1,13},{13,... | collective-permute-start | bytes 737288 | tf_op jit(solution)/shard_map/ppermute | solution.py:19
  135.2 38.0 %collective-permute-start.18 = (bf16[4,128,768]{2,1,0:T(8,128)(2,1)S(1)}, bf16[4,128,768]{2,1,0:T(8,128)(2,1)S(1)}, u32[]{:S(2)}, u32[]{:S(2)}) collective-permute-start(bf16[4,128,768]{2,1,0:T(8,128)(2,1)S(1)} %pad_maximum_fusion.1), channel_id=1, source_target_pairs={{0,84},{1,85},{2,86},{3,87},{4,88},{5,89},{6,90},{7,91},{8,92},{9,... | collective-permute-start | bytes 2359304 | tf_op jit(solution)/shard_map/ppermute | solution.py:211
  139.2 11.2 %collective-permute-start.14 = (bf16[160,768]{1,0:T(8,128)(2,1)S(1)}, bf16[160,768]{1,0:T(8,128)(2,1)S(1)}, u32[]{:S(2)}, u32[]{:S(2)}) collective-permute-start(bf16[160,768]{1,0:T(8,128)(2,1)S(1)} %block.22), channel_id=1, source_target_pairs={{0,12},{12,24},{24,36},{36,48},{48,60},{60,72},{72,84},{1,13},{13,... | collective-permute-start | bytes 737288 | tf_op jit(solution)/shard_map/ppermute | solution.py:19
  146.8 11.6 %collective-permute-start.22 = (bf16[160,768]{1,0:T(8,128)(2,1)S(1)}, bf16[160,768]{1,0:T(8,128)(2,1)S(1)}, u32[]{:S(2)}, u32[]{:S(2)}) collective-permute-start(bf16[160,768]{1,0:T(8,128)(2,1)S(1)} %block.30), channel_id=1, source_target_pairs={{0,12},{12,24},{24,36},{36,48},{48,60},{60,72},{72,84},{1,13},{13,... | collective-permute-start | bytes 737288 | tf_op jit(solution)/shard_map/ppermute | solution.py:19
  152.3 10.8 %collective-permute-start.15 = (bf16[160,768]{1,0:T(8,128)(2,1)S(1)}, bf16[160,768]{1,0:T(8,128)(2,1)S(1)}, u32[]{:S(2)}, u32[]{:S(2)}) collective-permute-start(bf16[160,768]{1,0:T(8,128)(2,1)S(1)} %block.23), channel_id=1, source_target_pairs={{0,12},{12,24},{24,36},{36,48},{48,60},{60,72},{72,84},{1,13},{13,... | collective-permute-start | bytes 737288 | tf_op jit(solution)/shard_map/ppermute | solution.py:19
  160.2 10.5 %collective-permute-start.23 = (bf16[160,768]{1,0:T(8,128)(2,1)S(1)}, bf16[160,768]{1,0:T(8,128)(2,1)S(1)}, u32[]{:S(2)}, u32[]{:S(2)}) collective-permute-start(bf16[160,768]{1,0:T(8,128)(2,1)S(1)} %block.31), channel_id=1, source_target_pairs={{0,12},{12,24},{24,36},{36,48},{48,60},{60,72},{72,84},{1,13},{13,... | collective-permute-start | bytes 737288 | tf_op jit(solution)/shard_map/ppermute | solution.py:19
  163.7 12.3 %collective-permute-start.16 = (bf16[160,768]{1,0:T(8,128)(2,1)S(1)}, bf16[160,768]{1,0:T(8,128)(2,1)S(1)}, u32[]{:S(2)}, u32[]{:S(2)}) collective-permute-start(bf16[160,768]{1,0:T(8,128)(2,1)S(1)} %block.24), channel_id=1, source_target_pairs={{0,12},{12,24},{24,36},{36,48},{48,60},{60,72},{72,84},{1,13},{13,... | collective-permute-start | bytes 737288 | tf_op jit(solution)/shard_map/ppermute | solution.py:19
  171.3 9.9 %collective-permute-start.24 = (bf16[160,768]{1,0:T(8,128)(2,1)S(1)}, bf16[160,768]{1,0:T(8,128)(2,1)S(1)}, u32[]{:S(2)}, u32[]{:S(2)}) collective-permute-start(bf16[160,768]{1,0:T(8,128)(2,1)S(1)} %block.32), channel_id=1, source_target_pairs={{0,12},{12,24},{24,36},{36,48},{48,60},{60,72},{72,84},{1,13},{13,... | collective-permute-start | bytes 737288 | tf_op jit(solution)/shard_map/ppermute | solution.py:19
  176.5 9.3 %collective-permute-start.25 = (bf16[160,768]{1,0:T(8,128)(2,1)S(1)}, bf16[160,768]{1,0:T(8,128)(2,1)S(1)}, u32[]{:S(2)}, u32[]{:S(2)}) collective-permute-start(bf16[160,768]{1,0:T(8,128)(2,1)S(1)} %block.27), channel_id=1, source_target_pairs={{0,12},{12,24},{24,36},{36,48},{48,60},{60,72},{72,84},{1,13},{13,... | collective-permute-start | bytes 737288 | tf_op jit(solution)/shard_map/ppermute | solution.py:19
  181.7 9.3 %collective-permute-start.26 = (bf16[160,768]{1,0:T(8,128)(2,1)S(1)}, bf16[160,768]{1,0:T(8,128)(2,1)S(1)}, u32[]{:S(2)}, u32[]{:S(2)}) collective-permute-start(bf16[160,768]{1,0:T(8,128)(2,1)S(1)} %block.33), channel_id=1, source_target_pairs={{0,12},{12,24},{24,36},{36,48},{48,60},{60,72},{72,84},{1,13},{13,... | collective-permute-start | bytes 737288 | tf_op jit(solution)/shard_map/ppermute | solution.py:19
where the time goes:
time: 193 us
  waiting for transfers between devices  76.7 us (40%)
  starting transfers between devices  57.5 us (30%)
  blocking collectives  36.9 us (19%)
  Pallas kernels  19.1 us (10%)
    ppermute x18, waiting for transfers between devices, moved(): lax.ppermute(block, axis, [(i, i + distance) for i in devices if i + dist...  56.9 us
    all_gather x1, blocking collectives, gathered(): lax.all_gather(shard.reshape(1, taps * rows, width), 'seq', axis=0, tiled...  36.9 us
    ppermute x18, starting transfers between devices, moved(): lax.ppermute(block, axis, [(i, i + distance) for i in devices if i + dist...  35.3 us
    ppermute x8, starting transfers between devices, shifted(): lax.ppermute(block, axis, [(i, (i + distance) % count) for i in range(cou...  21.5 us
    ppermute x8, waiting for transfers between devices, shifted(): lax.ppermute(block, axis, [(i, (i + distance) % count) for i in range(cou...  19.8 us
    pallas_call x18, Pallas kernels, block(): pl.pallas_call(lambda *refs: block_kernel(turn, pairs, segments, taps, le...  15.4 us
  transfers between devices with their start and end apart: 27, of which 23 were waited for; matrix products, arithmetic and copies ran while one was open for 0% of the time, Pallas kernels for 8%

commit v1 on v0

--- a/solution.py
+++ b/solution.py
@@ -108,13 +108,14 @@
     return out.reshape(taps * blocks * rows, width)
 
 
-def block_kernel(turn, pairs, segments, taps, length, halo, has_own, has_incoming, has_join, info_ref, *refs):
+def block_kernel(turn, pairs, segments, taps, length, halo, trim, has_own, has_incoming, has_join, info_ref, *refs):
     refs = list(refs)
     incoming_ref = refs.pop(0) if has_incoming else None
     own_ref = refs.pop(0) if has_own else None
     join_ref = refs.pop(0) if has_join else None
     kernel_ref, gain_ref, bias_ref, out_ref, cat_ref = refs
-    extent, width = out_ref.shape
+    extent, width = cat_ref.shape[0], out_ref.shape[1]
+    cut = (extent - out_ref.shape[0]) // 2
     segment = info_ref[0]
     pair = turn - segment
 
@@ -126,7 +127,7 @@
         else:
             wide = (own_ref if has_own else incoming_ref)[...].astype(jnp.float32)
         stat = jnp.mean(wide * wide, axis=-1, keepdims=True)
-        place = info_ref[1] + lax.broadcasted_iota(jnp.int32, (extent, 1), 0)
+        place = info_ref[1] + trim + lax.broadcasted_iota(jnp.int32, (extent, 1), 0)
         inside = jnp.logical_and(place >= 0, place < length)
         normed = wide * lax.rsqrt(stat + 1e-06) * gain_ref[...]
         normed = jnp.where(inside, normed, 0.0)
@@ -136,24 +137,25 @@
             cat_ref[:, tap * width : (tap + 1) * width] = turned.astype(jnp.bfloat16)
         total = jnp.dot(cat_ref[...], kernel_ref[...], preferred_element_type=jnp.float32)
         lifted = wide + jax.nn.gelu(total + bias_ref[...], approximate=True)
-        out_ref[...] = lifted.astype(jnp.bfloat16)
+        out_ref[...] = lifted[cut : extent - cut].astype(jnp.bfloat16)
         if has_join:
 
             @pl.when(segment == segments - 1)
             def _():
-                inner = lifted[halo : extent - halo] + join_ref[...].astype(jnp.float32)
-                out_ref[halo : extent - halo, :] = inner.astype(jnp.bfloat16)
-
-
-def block(info, incoming, own, join, kernel, gain, bias, turn, pairs, segments, taps, length, halo):
+                inner = lifted[halo - trim : extent - halo + trim] + join_ref[...].astype(jnp.float32)
+                edge = halo - trim - cut
+                out_ref[edge : out_ref.shape[0] - edge, :] = inner.astype(jnp.bfloat16)
+
+
+def block(info, incoming, own, join, kernel, gain, bias, turn, pairs, segments, taps, length, halo, trim, trim_out):
     given = [a for a in (incoming, own, join) if a is not None]
     extent, width = (incoming if incoming is not None else own).shape
     vmem = pl.BlockSpec(memory_space=pltpu.VMEM)
     return pl.pallas_call(
         lambda *refs: block_kernel(
-            turn, pairs, segments, taps, length, halo, own is not None, incoming is not None, join is not None, *refs
+            turn, pairs, segments, taps, length, halo, trim, own is not None, incoming is not None, join is not None, *refs
         ),
-        out_shape=jax.ShapeDtypeStruct((extent, width), jnp.bfloat16),
+        out_shape=jax.ShapeDtypeStruct((extent - 2 * (trim_out - trim), width), jnp.bfloat16),
         in_specs=[pl.BlockSpec(memory_space=pltpu.SMEM)] + [vmem] * (len(given) + 3),
         out_specs=vmem,
         scratch_shapes=[pltpu.VMEM((extent, taps * width), jnp.bfloat16)],
@@ -193,14 +195,17 @@
     kept = [None] * micro_count
     early = []
     joined = None
+    trims = [max(0, turn - pairs + 1) * (taps // 2) // 8 * 8 for turn in range(turns)]
     for turn in range(turns):
+        trim, trim_out = trims[turn], trims[min(turn + 1, turns - 1)]
+        hops = [(s, s + 1) for s in range(segments - 1) if 0 <= turn - s < pairs]
         for lane in range(PAIR):
             own = extended[turn * PAIR + lane] if turn < pairs else None
             join = joined[(turn - segments + 1) * PAIR + lane] if turn >= segments - 1 else None
-            out = block(info, incoming[lane], own, join, kernel, norm_gain, conv_bias, turn, pairs, segments, taps, length, halo)
+            out = block(info, incoming[lane], own, join, kernel, norm_gain, conv_bias, turn, pairs, segments, taps, length, halo, trim, trim_out)
             if turn < turns - 1:
-                incoming[lane] = moved(out, "segment", 1)
-            inner = out[halo : halo + rows]
+                incoming[lane] = lax.ppermute(out, "segment", hops)
+            inner = out[halo - trim_out : halo - trim_out + rows]
             if turn < pairs:
                 early.append(inner)
             for which in range(pairs):

time: 193 us -> 179 us (0.927)
  the two profiles are of different devices: /device:TPU:38 before, /device:TPU:126 now
where the time goes in v1:
time: 179 us
  waiting for transfers between devices  81.3 us (45%)
  starting transfers between devices  41.9 us (23%)
  blocking collectives  33.8 us (19%)
  Pallas kernels  18.9 us (11%)
    all_gather x1, blocking collectives, gathered(): lax.all_gather(shard.reshape(1, taps * rows, width), 'seq', axis=0, tiled...  33.8 us
    ppermute x16, waiting for transfers between devices, per_device(): incoming[lane] = lax.ppermute(out, 'segment', hops)  30.5 us
    ppermute x1, waiting for transfers between devices, per_device(): joined = lax.ppermute(jnp.stack(early), 'segment', [(0, segments - 1)])  26.7 us
    ppermute x8, starting transfers between devices, shifted(): lax.ppermute(block, axis, [(i, (i + distance) % count) for i in range(cou...  21.5 us
    ppermute x8, waiting for transfers between devices, shifted(): lax.ppermute(block, axis, [(i, (i + distance) % count) for i in range(cou...  19.9 us
    pallas_call x18, Pallas kernels, block(): pl.pallas_call(lambda *refs: block_kernel(turn, pairs, segments, taps, le...  15.2 us
    ppermute x16, starting transfers between devices, per_device(): incoming[lane] = lax.ppermute(out, 'segment', hops)  13.3 us
    ppermute x2, starting transfers between devices, moved(): lax.ppermute(block, axis, [(i, i + distance) for i in devices if i + dist...  5.87 us
  transfers between devices with their start and end apart: 27, of which 12 were waited for; matrix products, arithmetic and copies ran while one was open for 0% of the time, Pallas kernels for 7%

profile of v1, /device:TPU:126, one launch (start us, length us, event | category | flops | bytes accessed | tf_op | source)
XLA Modules:
  0.0 178.6 jit_solution(2304788531499105859)
XLA Ops:
  0.2 33.8 %all_gather.3.refs_0_ = bf16[12,40,768]{2,1,0:T(8,128)(2,1)S(1)} all-gather(bf16[1,40,768]{2,1,0:T(8,128)(2,1)} %bitcast.78), channel_id=1, replica_groups=mesh['x'=4,'core'=2,'segment'=8,'seq'=12] {'seq'}, dimensions={0}, use_global_device_ids=true | all-gather | bytes 798720 | tf_op jit(solution)/shard_map/all_gather | solution.py:71
  34.0 2.4 %collective-permute-start.2 = (bf16[6,40,768]{2,1,0:T(8,128)(2,1)S(1)}, bf16[6,40,768]{2,1,0:T(8,128)(2,1)S(1)}, u32[]{:S(2)}, u32[]{:S(2)}) collective-permute-start(bf16[6,40,768]{2,1,0:T(8,128)(2,1)S(1)} %get-tuple-element.50), channel_id=1, source_target_pairs={{0,192},{192,384},{384,576},{576,0},{1,193},{193,385},{385,577},{5... | collective-permute-start | bytes 1105928 | tf_op jit(solution)/shard_map/ppermute | solution.py:14
  36.4 3.5 %collective-permute-start.3 = (bf16[6,40,768]{2,1,0:T(8,128)(2,1)S(1)}, bf16[6,40,768]{2,1,0:T(8,128)(2,1)S(1)}, u32[]{:S(2)}, u32[]{:S(2)}) collective-permute-start(bf16[6,40,768]{2,1,0:T(8,128)(2,1)S(1)} %get-tuple-element.49), channel_id=1, source_target_pairs={{0,192},{192,384},{384,576},{576,0},{1,193},{193,385},{385,577},{5... | collective-permute-start | bytes 1105928 | tf_op jit(solution)/shard_map/ppermute | solution.py:14
  40.0 2.4 %collective-permute-start.4 = (bf16[6,40,768]{2,1,0:T(8,128)(2,1)S(1)}, bf16[6,40,768]{2,1,0:T(8,128)(2,1)S(1)}, u32[]{:S(2)}, u32[]{:S(2)}) collective-permute-start(bf16[6,40,768]{2,1,0:T(8,128)(2,1)S(1)} %get-tuple-element.50), channel_id=1, source_target_pairs={{0,576},{192,0},{384,192},{576,384},{1,577},{193,1},{385,193},{577... | collective-permute-start | bytes 1105928 | tf_op jit(solution)/shard_map/ppermute | solution.py:14
  42.4 3.5 %collective-permute-start.5 = (bf16[6,40,768]{2,1,0:T(8,128)(2,1)S(1)}, bf16[6,40,768]{2,1,0:T(8,128)(2,1)S(1)}, u32[]{:S(2)}, u32[]{:S(2)}) collective-permute-start(bf16[6,40,768]{2,1,0:T(8,128)(2,1)S(1)} %get-tuple-element.49), channel_id=1, source_target_pairs={{0,576},{192,0},{384,192},{576,384},{1,577},{193,1},{385,193},{577... | collective-permute-start | bytes 1105928 | tf_op jit(solution)/shard_map/ppermute | solution.py:14
  45.9 3.1 %collective-permute-done.3.refs_2_ = bf16[6,40,768]{2,1,0:T(8,128)(2,1)S(1)} collective-permute-done((bf16[6,40,768]{2,1,0:T(8,128)(2,1)S(1)}, bf16[6,40,768]{2,1,0:T(8,128)(2,1)S(1)}, u32[]{:S(2)}, u32[]{:S(2)}) %collective-permute-start.3) | collective-permute-done | bytes 368672 | tf_op jit(solution)/shard_map/ppermute | solution.py:14
  49.0 2.6 %collective-permute-done.4.refs_3_ = bf16[6,40,768]{2,1,0:T(8,128)(2,1)S(1)} collective-permute-done((bf16[6,40,768]{2,1,0:T(8,128)(2,1)S(1)}, bf16[6,40,768]{2,1,0:T(8,128)(2,1)S(1)}, u32[]{:S(2)}, u32[]{:S(2)}) %collective-permute-start.4) | collective-permute-done | bytes 368672 | tf_op jit(solution)/shard_map/ppermute | solution.py:14
  51.7 3.9 %collective-permute-done.5.refs_4_ = bf16[6,40,768]{2,1,0:T(8,128)(2,1)S(1)} collective-permute-done((bf16[6,40,768]{2,1,0:T(8,128)(2,1)S(1)}, bf16[6,40,768]{2,1,0:T(8,128)(2,1)S(1)}, u32[]{:S(2)}, u32[]{:S(2)}) %collective-permute-start.5) | collective-permute-done | bytes 368672 | tf_op jit(solution)/shard_map/ppermute | solution.py:14
  56.6 1.9 %collective-permute-start.8 = (bf16[36,40,768]{2,1,0:T(8,128)(2,1)S(1)}, bf16[36,40,768]{2,1,0:T(8,128)(2,1)S(1)}, u32[]{:S(2)}, u32[]{:S(2)}) collective-permute-start(bf16[36,40,768]{2,1,0:T(8,128)(2,1)S(1)} %merge.2), channel_id=1, source_target_pairs={{0,96},{96,0},{1,97},{97,1},{2,98},{98,2},{3,99},{99,3},{4,100},{1... | collective-permute-start | bytes 6635528 | tf_op jit(solution)/shard_map/ppermute | solution.py:14
  58.5 2.2 %collective-permute-start.6 = (bf16[6,40,768]{2,1,0:T(8,128)(2,1)S(1)}, bf16[6,40,768]{2,1,0:T(8,128)(2,1)S(1)}, u32[]{:S(2)}, u32[]{:S(2)}) collective-permute-start(bf16[6,40,768]{2,1,0:T(8,128)(2,1)S(1)} %collective-permute-done.2.refs_1_), channel_id=1, source_target_pairs={{0,192},{192,384},{384,576},{576,0},{1,193},{193,385},{385,577},{5... | collective-permute-start | bytes 1105928 | tf_op jit(solution)/shard_map/ppermute | solution.py:14
  60.7 3.7 %collective-permute-start.7 = (bf16[6,40,768]{2,1,0:T(8,128)(2,1)S(1)}, bf16[6,40,768]{2,1,0:T(8,128)(2,1)S(1)}, u32[]{:S(2)}, u32[]{:S(2)}) collective-permute-start(bf16[6,40,768]{2,1,0:T(8,128)(2,1)S(1)} %collective-permute-done.5.refs_4_), channel_id=1, source_target_pairs={{0,576},{192,0},{384,192},{576,384},{1,577},{193,1},{385,193},{577... | collective-permute-start | bytes 1105928 | tf_op jit(solution)/shard_map/ppermute | solution.py:14
  64.4 7.0 %collective-permute-done.6.refs_0_ = bf16[6,40,768]{2,1,0:T(8,128)(2,1)S(1)} collective-permute-done((bf16[6,40,768]{2,1,0:T(8,128)(2,1)S(1)}, bf16[6,40,768]{2,1,0:T(8,128)(2,1)S(1)}, u32[]{:S(2)}, u32[]{:S(2)}) %collective-permute-start.6) | collective-permute-done | bytes 368672 | tf_op jit(solution)/shard_map/ppermute | solution.py:14
  71.4 3.1 %collective-permute-done.7.refs_1_ = bf16[6,40,768]{2,1,0:T(8,128)(2,1)S(1)} collective-permute-done((bf16[6,40,768]{2,1,0:T(8,128)(2,1)S(1)}, bf16[6,40,768]{2,1,0:T(8,128)(2,1)S(1)}, u32[]{:S(2)}, u32[]{:S(2)}) %collective-permute-start.7) | collective-permute-done | bytes 368672 | tf_op jit(solution)/shard_map/ppermute | solution.py:14
  74.9 1.9 %collective-permute-start.9 = (bf16[12,40,768]{2,1,0:T(8,128)(2,1)S(1)}, bf16[12,40,768]{2,1,0:T(8,128)(2,1)S(1)}, u32[]{:S(2)}, u32[]{:S(2)}) collective-permute-start(bf16[12,40,768]{2,1,0:T(8,128)(2,1)S(1)} %merge.3), channel_id=1, source_target_pairs={{0,96},{96,0},{1,97},{97,1},{2,98},{98,2},{3,99},{99,3},{4,100},{1... | collective-permute-start | bytes 2211848 | tf_op jit(solution)/shard_map/ppermute | solution.py:14
  76.8 3.4 %collective-permute-start = (bf16[4,16,768]{2,1,0:T(8,128)(2,1)S(1)}, bf16[4,16,768]{2,1,0:T(8,128)(2,1)S(1)}, u32[]{:S(2)}, u32[]{:S(2)}) collective-permute-start(bf16[4,16,768]{2,1,0:T(8,128)(2,1)S(1)} %get-tuple-element.47), channel_id=1, source_target_pairs={{0,1},{1,2},{2,3},{3,4},{4,5},{5,6},{6,7},{7,8},{8,9},{9,10},{10,1... | collective-permute-start | bytes 294920 | tf_op jit(solution)/shard_map/ppermute | solution.py:19
  80.2 2.5 %collective-permute-start.1 = (bf16[4,16,768]{2,1,0:T(8,128)(2,1)S(1)}, bf16[4,16,768]{2,1,0:T(8,128)(2,1)S(1)}, u32[]{:S(2)}, u32[]{:S(2)}) collective-permute-start(bf16[4,16,768]{2,1,0:T(8,128)(2,1)S(1)} %get-tuple-element.48), channel_id=1, source_target_pairs={{1,0},{2,1},{3,2},{4,3},{5,4},{6,5},{7,6},{8,7},{9,8},{10,9},{11,1... | collective-permute-start | bytes 294920 | tf_op jit(solution)/shard_map/ppermute | solution.py:19
  82.7 1.5 collective-permute-done
  84.2 2.8 %collective-permute-done.1 = bf16[4,16,768]{2,1,0:T(8,128)(2,1)S(1)} collective-permute-done((bf16[4,16,768]{2,1,0:T(8,128)(2,1)S(1)}, bf16[4,16,768]{2,1,0:T(8,128)(2,1)S(1)}, u32[]{:S(2)}, u32[]{:S(2)}) %collective-permute-start.1) | collective-permute-done | bytes 98336 | tf_op jit(solution)/shard_map/ppermute | solution.py:19
  87.2 2.4 %assemble.1 = bf16[5,96,8,768]{3,2,1,0:T(8,128)(2,1)S(1)} custom-call(s32[8]{0:T(128)S(1)} %pad_add_fusion.1.refs_0_, bf16[12,5,8,768]{3,2,1,0:T(8,128)(2,1)S(1)} %bitcast.67, bf16[6,5,8,768]{3,2,1,0:T(8,128)(2,1)S(1)} %bitcast.69, bf16[6,5,8,768]{3,2,1,0:T(8,128)(2,1)S(1)} %bitcast.70, bf16[6,5,8,768]{3,2,1,0:T(8,128)(2,1)S(1)} %bitcast.71, ...), custom_call_target="tpu_custom_call" | custom-call | tf_op jit(solution)/shard_map/assemble/pallas_call | solution.py:98
  100.0 1.3 collective-permute-start.18
  106.9 1.3 collective-permute-start.16
  108.8 1.3 collective-permute-start.24
  110.1 26.7 %collective-permute-done.18 = bf16[4,128,768]{2,1,0:T(8,128)(2,1)S(1)} collective-permute-done((bf16[4,128,768]{2,1,0:T(8,128)(2,1)S(1)}, bf16[4,128,768]{2,1,0:T(8,128)(2,1)S(1)}, u32[]{:S(2)}, u32[]{:S(2)}) %collective-permute-start.18) | collective-permute-done | bytes 786464 | tf_op jit(solution)/shard_map/ppermute | solution.py:216
  136.8 25.7 %collective-permute-done.16.refs_1_ = bf16[144,768]{1,0:T(8,128)(2,1)S(1)} collective-permute-done((bf16[144,768]{1,0:T(8,128)(2,1)S(1)}, bf16[144,768]{1,0:T(8,128)(2,1)S(1)}, u32[]{:S(2)}, u32[]{:S(2)}) %collective-permute-start.16) | collective-permute-done | bytes 221216 | tf_op jit(solution)/shard_map/ppermute | solution.py:207
  162.5 1.8 %block.27 = bf16[144,768]{1,0:T(8,128)(2,1)S(1)} custom-call(s32[2]{0:T(128)S(1)} %pad_add_fusion.refs_0_, bf16[144,768]{1,0:T(8,128)(2,1)S(1)} %collective-permute-done.16.refs_1_, bf16[128,768]{1,0:T(8,128)(2,1)S(1)} %get-tuple-element.46.refs_2_, bf16[3840,768]{1,0:T(8,128)(2,1)S(1)} %bitcast.63, f32[1,768]{1,0:T(1,128)S(1)} %copy-done, ...), custom_call_target="tpu_custom_call" | custom-call | flops 849346560 | bytes 5898240 | tf_op jit(solution)/shard_map/block/pallas_call | solution.py:154
  164.3 1.3 collective-permute-start.25
  166.1 1.8 %block.33 = bf16[144,768]{1,0:T(8,128)(2,1)S(1)} custom-call(s32[2]{0:T(128)S(1)} %pad_add_fusion.refs_0_, bf16[144,768]{1,0:T(8,128)(2,1)S(1)} %collective-permute-done.24.refs_1_, bf16[128,768]{1,0:T(8,128)(2,1)S(1)} %get-tuple-element.45.refs_2_, bf16[3840,768]{1,0:T(8,128)(2,1)S(1)} %bitcast.64, f32[1,768]{1,0:T(1,128)S(1)} %copy-done, ...), custom_call_target="tpu_custom_call" | custom-call | flops 849346560 | bytes 5898240 | tf_op jit(solution)/shard_map/block/pallas_call | solution.py:154
  167.9 1.3 collective-permute-start.26
  169.4 2.7 %collective-permute-done.25.refs_1_ = bf16[144,768]{1,0:T(8,128)(2,1)S(1)} collective-permute-done((bf16[144,768]{1,0:T(8,128)(2,1)S(1)}, bf16[144,768]{1,0:T(8,128)(2,1)S(1)}, u32[]{:S(2)}, u32[]{:S(2)}) %collective-permute-start.25) | collective-permute-done | bytes 221216 | tf_op jit(solution)/shard_map/ppermute | solution.py:207
  172.1 1.8 %block.34 = bf16[144,768]{1,0:T(8,128)(2,1)S(1)} custom-call(s32[2]{0:T(128)S(1)} %pad_add_fusion.refs_0_, bf16[144,768]{1,0:T(8,128)(2,1)S(1)} %collective-permute-done.25.refs_1_, bf16[128,768]{1,0:T(8,128)(2,1)S(1)} %get-tuple-element.43.refs_2_, bf16[3840,768]{1,0:T(8,128)(2,1)S(1)} %bitcast.65, f32[1,768]{1,0:T(1,128)S(1)} %copy-done, ...), custom_call_target="tpu_custom_call" | custom-call | flops 849346560 | bytes 5898240 | tf_op jit(solution)/shard_map/block/pallas_call | solution.py:154
  174.1 1.6 collective-permute-done.26.refs_1_
  175.7 1.8 %block.35 = bf16[144,768]{1,0:T(8,128)(2,1)S(1)} custom-call(s32[2]{0:T(128)S(1)} %pad_add_fusion.refs_0_, bf16[144,768]{1,0:T(8,128)(2,1)S(1)} %collective-permute-done.26.refs_1_, bf16[128,768]{1,0:T(8,128)(2,1)S(1)} %get-tuple-element.44.refs_2_, bf16[3840,768]{1,0:T(8,128)(2,1)S(1)} %bitcast.66, f32[1,768]{1,0:T(1,128)S(1)} %copy-done, ...), custom_call_target="tpu_custom_call" | custom-call | flops 849346560 | bytes 5898240 | tf_op jit(solution)/shard_map/block/pallas_call | solution.py:154
  (68 shorter events, 19.8 us)
Async XLA Ops:
  34.0 11.9 %collective-permute-start.2 = (bf16[6,40,768]{2,1,0:T(8,128)(2,1)S(1)}, bf16[6,40,768]{2,1,0:T(8,128)(2,1)S(1)}, u32[]{:S(2)}, u32[]{:S(2)}) collective-permute-start(bf16[6,40,768]{2,1,0:T(8,128)(2,1)S(1)} %get-tuple-element.50), channel_id=1, source_target_pairs={{0,192},{192,384},{384,576},{576,0},{1,193},{193,385},{385,577},{5... | collective-permute-start | bytes 1105928 | tf_op jit(solution)/shard_map/ppermute | solution.py:14
  36.4 40.4 %copy-start.2 = (bf16[1,4,128,768]{3,2,1,0:T(8,128)(2,1)S(1)}, bf16[1,4,128,768]{3,2,1,0:T(8,128)(2,1)}, u32[]{:S(2)}) copy-start(bf16[1,4,128,768]{3,2,1,0:T(8,128)(2,1)} %param.4) | copy-start | bytes 2359300
  36.4 12.6 %collective-permute-start.3 = (bf16[6,40,768]{2,1,0:T(8,128)(2,1)S(1)}, bf16[6,40,768]{2,1,0:T(8,128)(2,1)S(1)}, u32[]{:S(2)}, u32[]{:S(2)}) collective-permute-start(bf16[6,40,768]{2,1,0:T(8,128)(2,1)S(1)} %get-tuple-element.49), channel_id=1, source_target_pairs={{0,192},{192,384},{384,576},{576,0},{1,193},{193,385},{385,577},{5... | collective-permute-start | bytes 1105928 | tf_op jit(solution)/shard_map/ppermute | solution.py:14
  40.0 11.7 %collective-permute-start.4 = (bf16[6,40,768]{2,1,0:T(8,128)(2,1)S(1)}, bf16[6,40,768]{2,1,0:T(8,128)(2,1)S(1)}, u32[]{:S(2)}, u32[]{:S(2)}) collective-permute-start(bf16[6,40,768]{2,1,0:T(8,128)(2,1)S(1)} %get-tuple-element.50), channel_id=1, source_target_pairs={{0,576},{192,0},{384,192},{576,384},{1,577},{193,1},{385,193},{577... | collective-permute-start | bytes 1105928 | tf_op jit(solution)/shard_map/ppermute | solution.py:14
  42.4 13.2 %collective-permute-start.5 = (bf16[6,40,768]{2,1,0:T(8,128)(2,1)S(1)}, bf16[6,40,768]{2,1,0:T(8,128)(2,1)S(1)}, u32[]{:S(2)}, u32[]{:S(2)}) collective-permute-start(bf16[6,40,768]{2,1,0:T(8,128)(2,1)S(1)} %get-tuple-element.49), channel_id=1, source_target_pairs={{0,576},{192,0},{384,192},{576,384},{1,577},{193,1},{385,193},{577... | collective-permute-start | bytes 1105928 | tf_op jit(solution)/shard_map/ppermute | solution.py:14
  56.6 30.6 %collective-permute-start.8 = (bf16[36,40,768]{2,1,0:T(8,128)(2,1)S(1)}, bf16[36,40,768]{2,1,0:T(8,128)(2,1)S(1)}, u32[]{:S(2)}, u32[]{:S(2)}) collective-permute-start(bf16[36,40,768]{2,1,0:T(8,128)(2,1)S(1)} %merge.2), channel_id=1, source_target_pairs={{0,96},{96,0},{1,97},{97,1},{2,98},{98,2},{3,99},{99,3},{4,100},{1... | collective-permute-start | bytes 6635528 | tf_op jit(solution)/shard_map/ppermute | solution.py:14
  58.5 12.9 %collective-permute-start.6 = (bf16[6,40,768]{2,1,0:T(8,128)(2,1)S(1)}, bf16[6,40,768]{2,1,0:T(8,128)(2,1)S(1)}, u32[]{:S(2)}, u32[]{:S(2)}) collective-permute-start(bf16[6,40,768]{2,1,0:T(8,128)(2,1)S(1)} %collective-permute-done.2.refs_1_), channel_id=1, source_target_pairs={{0,192},{192,384},{384,576},{576,0},{1,193},{193,385},{385,577},{5... | collective-permute-start | bytes 1105928 | tf_op jit(solution)/shard_map/ppermute | solution.py:14
  60.7 13.8 %collective-permute-start.7 = (bf16[6,40,768]{2,1,0:T(8,128)(2,1)S(1)}, bf16[6,40,768]{2,1,0:T(8,128)(2,1)S(1)}, u32[]{:S(2)}, u32[]{:S(2)}) collective-permute-start(bf16[6,40,768]{2,1,0:T(8,128)(2,1)S(1)} %collective-permute-done.5.refs_4_), channel_id=1, source_target_pairs={{0,576},{192,0},{384,192},{576,384},{1,577},{193,1},{385,193},{577... | collective-permute-start | bytes 1105928 | tf_op jit(solution)/shard_map/ppermute | solution.py:14
  74.9 12.3 %collective-permute-start.9 = (bf16[12,40,768]{2,1,0:T(8,128)(2,1)S(1)}, bf16[12,40,768]{2,1,0:T(8,128)(2,1)S(1)}, u32[]{:S(2)}, u32[]{:S(2)}) collective-permute-start(bf16[12,40,768]{2,1,0:T(8,128)(2,1)S(1)} %merge.3), channel_id=1, source_target_pairs={{0,96},{96,0},{1,97},{97,1},{2,98},{98,2},{3,99},{99,3},{4,100},{1... | collective-permute-start | bytes 2211848 | tf_op jit(solution)/shard_map/ppermute | solution.py:14
  76.8 7.4 %collective-permute-start = (bf16[4,16,768]{2,1,0:T(8,128)(2,1)S(1)}, bf16[4,16,768]{2,1,0:T(8,128)(2,1)S(1)}, u32[]{:S(2)}, u32[]{:S(2)}) collective-permute-start(bf16[4,16,768]{2,1,0:T(8,128)(2,1)S(1)} %get-tuple-element.47), channel_id=1, source_target_pairs={{0,1},{1,2},{2,3},{3,4},{4,5},{5,6},{6,7},{7,8},{8,9},{9,10},{10,1... | collective-permute-start | bytes 294920 | tf_op jit(solution)/shard_map/ppermute | solution.py:19
  80.2 6.8 %collective-permute-start.1 = (bf16[4,16,768]{2,1,0:T(8,128)(2,1)S(1)}, bf16[4,16,768]{2,1,0:T(8,128)(2,1)S(1)}, u32[]{:S(2)}, u32[]{:S(2)}) collective-permute-start(bf16[4,16,768]{2,1,0:T(8,128)(2,1)S(1)} %get-tuple-element.48), channel_id=1, source_target_pairs={{1,0},{2,1},{3,2},{4,3},{5,4},{6,5},{7,6},{8,7},{9,8},{10,9},{11,1... | collective-permute-start | bytes 294920 | tf_op jit(solution)/shard_map/ppermute | solution.py:19
  87.2 2.4 %copy-start = (f32[1,768]{1,0:T(1,128)S(1)}, f32[1,768]{1,0:T(1,128)}, u32[]{:S(2)}) copy-start(f32[1,768]{1,0:T(1,128)} %refs_4_.35) | copy-start | bytes 9220
  87.2 2.4 %copy-start.1 = (f32[1,768]{1,0:T(1,128)S(1)}, f32[1,768]{1,0:T(1,128)}, u32[]{:S(2)}) copy-start(f32[1,768]{1,0:T(1,128)} %refs_5_.11) | copy-start | bytes 9220
  90.2 2.0 %collective-permute-start.10 = (bf16[160,768]{1,0:T(8,128)(2,1)S(1)}, bf16[160,768]{1,0:T(8,128)(2,1)S(1)}, u32[]{:S(2)}, u32[]{:S(2)}) collective-permute-start(bf16[160,768]{1,0:T(8,128)(2,1)S(1)} %block.18), channel_id=1, source_target_pairs={{0,12},{1,13},{2,14},{3,15},{4,16},{5,17},{6,18},{7,19},{8,20},{9,... | collective-permute-start | bytes 737288 | tf_op jit(solution)/shard_map/ppermute | solution.py:207
  91.4 2.0 %collective-permute-start.17 = (bf16[160,768]{1,0:T(8,128)(2,1)S(1)}, bf16[160,768]{1,0:T(8,128)(2,1)S(1)}, u32[]{:S(2)}, u32[]{:S(2)}) collective-permute-start(bf16[160,768]{1,0:T(8,128)(2,1)S(1)} %block.25), channel_id=1, source_target_pairs={{0,12},{1,13},{2,14},{3,15},{4,16},{5,17},{6,18},{7,19},{8,20},{9,... | collective-permute-start | bytes 737288 | tf_op jit(solution)/shard_map/ppermute | solution.py:207
  92.7 2.0 %collective-permute-start.11 = (bf16[160,768]{1,0:T(8,128)(2,1)S(1)}, bf16[160,768]{1,0:T(8,128)(2,1)S(1)}, u32[]{:S(2)}, u32[]{:S(2)}) collective-permute-start(bf16[160,768]{1,0:T(8,128)(2,1)S(1)} %block.19), channel_id=1, source_target_pairs={{0,12},{12,24},{1,13},{13,25},{2,14},{14,26},{3,15},{15,27},{4,16}... | collective-permute-start | bytes 737288 | tf_op jit(solution)/shard_map/ppermute | solution.py:207
  94.0 2.0 %collective-permute-start.19 = (bf16[160,768]{1,0:T(8,128)(2,1)S(1)}, bf16[160,768]{1,0:T(8,128)(2,1)S(1)}, u32[]{:S(2)}, u32[]{:S(2)}) collective-permute-start(bf16[160,768]{1,0:T(8,128)(2,1)S(1)} %block.26), channel_id=1, source_target_pairs={{0,12},{12,24},{1,13},{13,25},{2,14},{14,26},{3,15},{15,27},{4,16}... | collective-permute-start | bytes 737288 | tf_op jit(solution)/shard_map/ppermute | solution.py:207
  95.2 2.0 %collective-permute-start.12 = (bf16[160,768]{1,0:T(8,128)(2,1)S(1)}, bf16[160,768]{1,0:T(8,128)(2,1)S(1)}, u32[]{:S(2)}, u32[]{:S(2)}) collective-permute-start(bf16[160,768]{1,0:T(8,128)(2,1)S(1)} %block.20), channel_id=1, source_target_pairs={{12,24},{24,36},{13,25},{25,37},{14,26},{26,38},{15,27},{27,39},{1... | collective-permute-start | bytes 737288 | tf_op jit(solution)/shard_map/ppermute | solution.py:207
  96.5 2.0 %collective-permute-start.20 = (bf16[160,768]{1,0:T(8,128)(2,1)S(1)}, bf16[160,768]{1,0:T(8,128)(2,1)S(1)}, u32[]{:S(2)}, u32[]{:S(2)}) collective-permute-start(bf16[160,768]{1,0:T(8,128)(2,1)S(1)} %block.28), channel_id=1, source_target_pairs={{12,24},{24,36},{13,25},{25,37},{14,26},{26,38},{15,27},{27,39},{1... | collective-permute-start | bytes 737288 | tf_op jit(solution)/shard_map/ppermute | solution.py:207
  97.8 3.6 %collective-permute-start.13 = (bf16[160,768]{1,0:T(8,128)(2,1)S(1)}, bf16[160,768]{1,0:T(8,128)(2,1)S(1)}, u32[]{:S(2)}, u32[]{:S(2)}) collective-permute-start(bf16[160,768]{1,0:T(8,128)(2,1)S(1)} %block.21), channel_id=1, source_target_pairs={{24,36},{36,48},{25,37},{37,49},{26,38},{38,50},{27,39},{39,51},{2... | collective-permute-start | bytes 737288 | tf_op jit(solution)/shard_map/ppermute | solution.py:207
  99.2 3.4 %collective-permute-start.21 = (bf16[160,768]{1,0:T(8,128)(2,1)S(1)}, bf16[160,768]{1,0:T(8,128)(2,1)S(1)}, u32[]{:S(2)}, u32[]{:S(2)}) collective-permute-start(bf16[160,768]{1,0:T(8,128)(2,1)S(1)} %block.29), channel_id=1, source_target_pairs={{24,36},{36,48},{25,37},{37,49},{26,38},{38,50},{27,39},{39,51},{2... | collective-permute-start | bytes 737288 | tf_op jit(solution)/shard_map/ppermute | solution.py:207
  100.0 36.7 %collective-permute-start.18 = (bf16[4,128,768]{2,1,0:T(8,128)(2,1)S(1)}, bf16[4,128,768]{2,1,0:T(8,128)(2,1)S(1)}, u32[]{:S(2)}, u32[]{:S(2)}) collective-permute-start(bf16[4,128,768]{2,1,0:T(8,128)(2,1)S(1)} %pad_maximum_fusion.1), channel_id=1, source_target_pairs={{0,84},{1,85},{2,86},{3,87},{4,88},{5,89},{6,90},{7,91},{8,92},{9,... | collective-permute-start | bytes 2359304 | tf_op jit(solution)/shard_map/ppermute | solution.py:216
  101.9 1.9 %collective-permute-start.14 = (bf16[144,768]{1,0:T(8,128)(2,1)S(1)}, bf16[144,768]{1,0:T(8,128)(2,1)S(1)}, u32[]{:S(2)}, u32[]{:S(2)}) collective-permute-start(bf16[144,768]{1,0:T(8,128)(2,1)S(1)} %block.22), channel_id=1, source_target_pairs={{36,48},{48,60},{37,49},{49,61},{38,50},{50,62},{39,51},{51,63},{4... | collective-permute-start | bytes 663560 | tf_op jit(solution)/shard_map/ppermute | solution.py:207
  103.1 1.9 %collective-permute-start.22 = (bf16[144,768]{1,0:T(8,128)(2,1)S(1)}, bf16[144,768]{1,0:T(8,128)(2,1)S(1)}, u32[]{:S(2)}, u32[]{:S(2)}) collective-permute-start(bf16[144,768]{1,0:T(8,128)(2,1)S(1)} %block.30), channel_id=1, source_target_pairs={{36,48},{48,60},{37,49},{49,61},{38,50},{50,62},{39,51},{51,63},{4... | collective-permute-start | bytes 663560 | tf_op jit(solution)/shard_map/ppermute | solution.py:207
  104.4 1.9 %collective-permute-start.15 = (bf16[144,768]{1,0:T(8,128)(2,1)S(1)}, bf16[144,768]{1,0:T(8,128)(2,1)S(1)}, u32[]{:S(2)}, u32[]{:S(2)}) collective-permute-start(bf16[144,768]{1,0:T(8,128)(2,1)S(1)} %block.23), channel_id=1, source_target_pairs={{48,60},{60,72},{49,61},{61,73},{50,62},{62,74},{51,63},{63,75},{5... | collective-permute-start | bytes 663560 | tf_op jit(solution)/shard_map/ppermute | solution.py:207
  105.7 2.6 %collective-permute-start.23 = (bf16[144,768]{1,0:T(8,128)(2,1)S(1)}, bf16[144,768]{1,0:T(8,128)(2,1)S(1)}, u32[]{:S(2)}, u32[]{:S(2)}) collective-permute-start(bf16[144,768]{1,0:T(8,128)(2,1)S(1)} %block.31), channel_id=1, source_target_pairs={{48,60},{60,72},{49,61},{61,73},{50,62},{62,74},{51,63},{63,75},{5... | collective-permute-start | bytes 663560 | tf_op jit(solution)/shard_map/ppermute | solution.py:207
  106.9 55.6 %collective-permute-start.16 = (bf16[144,768]{1,0:T(8,128)(2,1)S(1)}, bf16[144,768]{1,0:T(8,128)(2,1)S(1)}, u32[]{:S(2)}, u32[]{:S(2)}) collective-permute-start(bf16[144,768]{1,0:T(8,128)(2,1)S(1)} %block.24), channel_id=1, source_target_pairs={{60,72},{72,84},{61,73},{73,85},{62,74},{74,86},{63,75},{75,87},{6... | collective-permute-start | bytes 663560 | tf_op jit(solution)/shard_map/ppermute | solution.py:207
  108.8 57.3 %collective-permute-start.24 = (bf16[144,768]{1,0:T(8,128)(2,1)S(1)}, bf16[144,768]{1,0:T(8,128)(2,1)S(1)}, u32[]{:S(2)}, u32[]{:S(2)}) collective-permute-start(bf16[144,768]{1,0:T(8,128)(2,1)S(1)} %block.32), channel_id=1, source_target_pairs={{60,72},{72,84},{61,73},{73,85},{62,74},{74,86},{63,75},{75,87},{6... | collective-permute-start | bytes 663560 | tf_op jit(solution)/shard_map/ppermute | solution.py:207
  164.3 7.8 %collective-permute-start.25 = (bf16[144,768]{1,0:T(8,128)(2,1)S(1)}, bf16[144,768]{1,0:T(8,128)(2,1)S(1)}, u32[]{:S(2)}, u32[]{:S(2)}) collective-permute-start(bf16[144,768]{1,0:T(8,128)(2,1)S(1)} %block.27), channel_id=1, source_target_pairs={{72,84},{73,85},{74,86},{75,87},{76,88},{77,89},{78,90},{79,91},{8... | collective-permute-start | bytes 663560 | tf_op jit(solution)/shard_map/ppermute | solution.py:207
  167.9 7.8 %collective-permute-start.26 = (bf16[144,768]{1,0:T(8,128)(2,1)S(1)}, bf16[144,768]{1,0:T(8,128)(2,1)S(1)}, u32[]{:S(2)}, u32[]{:S(2)}) collective-permute-start(bf16[144,768]{1,0:T(8,128)(2,1)S(1)} %block.33), channel_id=1, source_target_pairs={{72,84},{73,85},{74,86},{75,87},{76,88},{77,89},{78,90},{79,91},{8... | collective-permute-start | bytes 663560 | tf_op jit(solution)/shard_map/ppermute | solution.py:207
